TPU v7x, 32 devices: a whole 2x2x4 slice. The times are simulated.
32 devices in a mesh: seq: 8 (over y, x, core), dp: 4 (over z).
Axes of the slice: x: 2, y: 2, z: 4, core: 2. Of those that a mesh axis runs over, the one named last changes fastest.
Arguments:
- layer_input: bfloat16 [4, 1024, 5120], P('dp', 'seq'), may hold values from -64 to 64, as said below
- out_grad: bfloat16 [4, 1024, 5120], P('dp', 'seq'), may hold values from -0.059814453 to 0.059814453
- w_query: bfloat16 [5120, 640], replicated, may hold values from -0.078125 to 0.078125
- w_key: bfloat16 [5120, 128], replicated, may hold values from -0.078125 to 0.078125
- w_value: bfloat16 [5120, 128], replicated, may hold values from -0.078125 to 0.078125
- w_output: bfloat16 [640, 5120], replicated, may hold values from -0.25 to 0.25
- block_mask: int32 [4, 8, 8], P('dp'), may hold values from 0 to 1, as said below
Outputs:
- grad_qkv: float32 [5120, 896], P(('seq', 'dp'))
- grad_output: float32 [640, 5120], P(('seq', 'dp'))
Inputs may be any that keep to these rules, and one draw needn't show every extreme that they name: `layer_input`: each position's entries are a bell-shaped or uniform body times a scale of that position; they may share a common direction, and some positions may repeat one strong vector. block_mask[r] has ones on its diagonal and zeros above it. The 8 blocks of sequence r form a shared prefix of at least half of them followed by a chosen branch and then a rejected branch, each of one block or more; a block attends every earlier or equal block of the prefix and of its own branch, and nothing else.
All inputs are finite; a program needn't handle non-finite values.
Results may differ from a plain program's by a relative error of at most 0.025.
The roundings to bfloat16 on the way count: a program that leaves them out, or rounds other values in their place, can miss the bound.
Values may be sent and summed in bfloat16 or wider, within the bound.
A program may use at most 128 MiB of HBM per device.

v0:
```python
import math

import jax
import jax.numpy as jnp
from jax import lax
from jax.sharding import PartitionSpec as P

BLOCK = 128


def allowed_block(mask_table, first_row, row_count, length):
    query_pos = first_row + jnp.arange(row_count, dtype=jnp.int32)
    key_pos = jnp.arange(length, dtype=jnp.int32)
    mask_rows = lax.dynamic_slice_in_dim(mask_table, first_row // BLOCK, row_count // BLOCK, 0)
    token_mask = jnp.repeat(jnp.repeat(mask_rows, BLOCK, axis=0), BLOCK, axis=1)
    same_block = query_pos[:, None] // BLOCK == key_pos[None, :] // BLOCK
    return (token_mask == 1) & (
        jnp.logical_not(same_block) | (key_pos[None, :] <= query_pos[:, None])
    )


def shards(layer_input, out_grad, w_query, w_key, w_value, w_output, block_mask):
    inputs_row = layer_input[0]
    grad_row = out_grad[0]
    mask_table = block_mask[0]
    tokens = inputs_row.shape[0]
    head_size = w_key.shape[1]
    group_heads = w_query.shape[1] // head_size
    scale = 1.0 / math.sqrt(head_size)
    queries = (
        jnp.dot(inputs_row, w_query, preferred_element_type=jnp.float32)
        .astype(jnp.bfloat16)
        .reshape(tokens, group_heads, head_size)
    )
    w_pair = jnp.concatenate([w_key, w_value], axis=1)
    kv_local = jnp.dot(inputs_row, w_pair, preferred_element_type=jnp.float32).astype(jnp.bfloat16)
    kv_all = lax.all_gather(kv_local, "seq", axis=0, tiled=True)
    length = kv_all.shape[0]
    key_rows = kv_all[:, :head_size]
    value_rows = kv_all[:, head_size:]
    first_row = lax.axis_index("seq") * tokens
    allowed = allowed_block(mask_table, first_row, tokens, length)
    attn_grad = (
        lax.dot_general(
            grad_row, w_output, (((1,), (1,)), ((), ())), preferred_element_type=jnp.float32
        )
        .astype(jnp.bfloat16)
        .reshape(tokens, group_heads, head_size)
    )
    scores = (
        jnp.einsum("tgh,sh->gts", queries, key_rows, preferred_element_type=jnp.float32) * scale
    )
    masked = jnp.where(allowed[None], scores, -jnp.inf)
    row_max = jnp.max(masked, axis=-1, keepdims=True)
    log_total = row_max + jnp.log(jnp.sum(jnp.exp(masked - row_max), axis=-1, keepdims=True))
    softmax_w = jnp.exp(masked - log_total)
    weights_b = softmax_w.astype(jnp.bfloat16)
    attn_out = jnp.einsum(
        "gts,sh->tgh", weights_b, value_rows, preferred_element_type=jnp.float32
    ).astype(jnp.bfloat16)
    row_delta = jnp.einsum(
        "tgh,tgh->gt", attn_grad.astype(jnp.float32), attn_out.astype(jnp.float32)
    )
    prob_grad = jnp.einsum("tgh,sh->gts", attn_grad, value_rows, preferred_element_type=jnp.float32)
    score_grad = (softmax_w * (prob_grad - row_delta[..., None])).astype(jnp.bfloat16)
    query_grad = (
        jnp.einsum("gts,sh->tgh", score_grad, key_rows, preferred_element_type=jnp.float32) * scale
    ).astype(jnp.bfloat16)
    query_grad = query_grad.reshape(tokens, group_heads * head_size)
    key_term = (
        jnp.einsum("gts,tgh->sh", score_grad, queries, preferred_element_type=jnp.float32) * scale
    )
    value_term = jnp.einsum("gts,tgh->sh", weights_b, attn_grad, preferred_element_type=jnp.float32)
    kv_grads = lax.psum_scatter(
        jnp.concatenate([key_term, value_term], axis=1), "seq", scatter_dimension=0, tiled=True
    )
    grads_all = jnp.concatenate([query_grad, kv_grads.astype(jnp.bfloat16)], axis=1)
    attn_flat = attn_out.reshape(tokens, group_heads * head_size)
    contract_rows = (((0,), (0,)), ((), ()))
    inputs_cols, grad_cols = (
        lax.all_to_all(inputs_row, "seq", split_axis=1, concat_axis=0, tiled=True),
        lax.all_to_all(grad_row, "seq", split_axis=1, concat_axis=0, tiled=True),
    )
    grads_seq, attn_seq = (
        lax.all_gather(grads_all, "seq", axis=0, tiled=True),
        lax.all_gather(attn_flat, "seq", axis=0, tiled=True),
    )
    qkv_cols = lax.dot_general(
        inputs_cols, grads_seq, contract_rows, preferred_element_type=jnp.float32
    )
    out_cols = lax.dot_general(
        attn_seq, grad_cols, contract_rows, preferred_element_type=jnp.float32
    )
    out_heads = lax.all_to_all(out_cols, "seq", split_axis=0, concat_axis=1, tiled=True)
    qkv_grad, output_grad = (
        lax.psum_scatter(qkv_cols, "dp", scatter_dimension=0, tiled=True),
        lax.psum_scatter(out_heads, "dp", scatter_dimension=0, tiled=True),
    )
    return (qkv_grad, output_grad)


def solution(mesh):
    placed = (P("dp", "seq", None), P("dp", "seq", None), P(), P(), P(), P(), P("dp", None, None))
    return jax.shard_map(
        shards,
        mesh=mesh,
        in_specs=placed,
        out_specs=(P(("seq", "dp"), None), P(("seq", "dp"), None)),
        check_vma=False,
    )
```

profile of v0, /device:TPU:1, one launch (start us, length us, event | category | flops | bytes accessed | tf_op | source)
XLA Modules:
  0.0 233.0 jit_solution(2066719553764132672)
XLA Ops:
  7.3 5.5 %fusion.18 = bf16[128,640]{1,0:T(8,128)(2,1)S(1)} fusion(bf16[640,5120]{1,0:T(8,128)(2,1)} %param.12, bf16[1,128,5120]{2,1,0:T(8,128)(2,1)} %param.8), kind=kOutput, calls=%fused_computation.23 | convolution fusion | flops 838942720 | bytes 8028160 | tf_op jit(solution)/shard_map/dot_general | solution.py:44
  12.9 4.2 %fusion.15 = bf16[128,640]{1,0:T(8,128)(2,1)S(1)} fusion(bf16[5120,640]{1,0:T(8,128)(2,1)} %param.9, bf16[1,128,5120]{2,1,0:T(8,128)(2,1)S(1)} %copy-done), kind=kOutput, calls=%fused_computation.22 | convolution fusion | flops 838942720 | bytes 8028160 | tf_op jit(solution)/shard_map/dot_general | solution.py:31
  17.3 2.2 fusion.26
  19.5 11.4 %all_gather.9 = bf16[1024,256]{0,1:T(8,128)(2,1)S(1)} all-gather(bf16[128,256]{0,1:T(8,128)(2,1)S(1)} %fusion.26), channel_id=1, replica_groups=mesh['seq'=8,'dp'=4] {'seq'}, dimensions={0}, use_global_device_ids=true | all-gather | bytes 589824 | tf_op jit(solution)/shard_map/all_gather | solution.py:37
  30.9 0.7 compare_bitcast_fusion
  32.0 0.6 fusion.40
  32.9 0.6 convolution_bitcast_fusion.1
  33.5 1.3 fusion.35
  34.8 0.7 fusion.6
  36.0 1.1 pad_maximum_fusion
  37.6 35.4 %reduce-scatter.7.cloned.1.call-done = f32[128,256]{0,1:T(8,128)} async-done(((f32[1024,256]{0,1:T(8,128)}), f32[128,256]{0,1:T(8,128)}) %reduce-scatter.7.cloned.1.call-update) | async-done | bytes 131088 | tf_op jit(solution)/shard_map/reduce_scatter | solution.py:74
  73.0 0.9 convert_element_type.45
  73.9 0.7 pad_maximum_fusion.1
  74.7 0.7 all-gather.5.cloned.1.call-update
  75.4 1.4 copy.53
  76.8 4.4 %all-to-all-start = ((bf16[128,8,640]{0,2,1:T(8,128)(2,1)}), bf16[128,8,640]{0,2,1:T(8,128)(2,1)S(1)}, u32[]{:S(2)}, u32[]{:S(2)}) async-start(bf16[128,8,640]{0,2,1:T(8,128)(2,1)} %bitcast.23), calls=%async_computation.1 | async-start | bytes 2621440 | tf_op jit(solution)/shard_map/all_to_all | solution.py:81
  81.4 1.2 copy.55
  82.7 15.7 %all-to-all-done = bf16[128,8,640]{0,2,1:T(8,128)(2,1)S(1)} async-done(((bf16[128,8,640]{0,2,1:T(8,128)(2,1)}), bf16[128,8,640]{0,2,1:T(8,128)(2,1)S(1)}, u32[]{:S(2)}, u32[]{:S(2)}) %all-to-all-start) | async-done | bytes 1310752 | tf_op jit(solution)/shard_map/all_to_all | solution.py:81
  98.4 7.7 %all-to-all-start.1 = ((bf16[128,8,640]{2,0,1:T(8,128)(2,1)}), bf16[128,8,640]{2,0,1:T(8,128)(2,1)}, u32[]{:S(2)}, u32[]{:S(2)}) async-start(bf16[128,8,640]{2,0,1:T(8,128)(2,1)} %copy.55), calls=%async_computation.2 | async-start | bytes 2621440 | tf_op jit(solution)/shard_map/all_to_all | solution.py:82
  106.1 1.4 copy.54
  107.5 0.9 all-gather.3.cloned.1.call-done
  108.5 3.5 %convolution_bitcast_fusion = f32[640,896]{0,1:T(8,128)S(1)} fusion(bf16[1024,896]{0,1:T(8,128)(2,1)} %all-gather.3.cloned.1.call-done, bf16[1024,640]{1,0:T(8,128)(2,1)} %bitcast.108), kind=kOutput, calls=%fused_computation.11 | convolution fusion | flops 1174405120 | bytes 5439488 | tf_op jit(solution)/shard_map/dot_general | solution.py:88
  111.9 2.1 copy.76
  114.1 8.5 %all-to-all-done.1 = bf16[128,8,640]{2,0,1:T(8,128)(2,1)} async-done(((bf16[128,8,640]{2,0,1:T(8,128)(2,1)}), bf16[128,8,640]{2,0,1:T(8,128)(2,1)}, u32[]{:S(2)}, u32[]{:S(2)}) %all-to-all-start.1) | async-done | bytes 1310752 | tf_op jit(solution)/shard_map/all_to_all | solution.py:82
  122.6 14.1 %all-gather.5.cloned.1.call-done = bf16[1024,640]{0,1:T(8,128)(2,1)} async-done(((bf16[128,640]{0,1:T(8,128)(2,1)}), bf16[1024,640]{0,1:T(8,128)(2,1)}) %all-gather.5.cloned.1.call-update) | async-done | bytes 1310736 | tf_op jit(solution)/shard_map/all_gather | solution.py:86
  136.6 2.9 %fusion.41 = f32[8,80,640]{2,1,0:T(8,128)S(1)} fusion(bf16[8,80,1024]{2,1,0:T(8,128)(2,1)} %bitcast.113, bf16[1024,640,1]{1,0,2:T(8,128)(2,1)} %bitcast.32), kind=kOutput, calls=%fused_computation.54 | convolution fusion | flops 838860800 | bytes 4259840 | tf_op jit(solution)/shard_map/dot_general | solution.py:91
  139.5 23.9 %all_to_all.54 = f32[8,80,640]{2,1,0:T(8,128)S(1)} all-to-all(f32[8,80,640]{2,1,0:T(8,128)S(1)} %fusion.41), channel_id=1, replica_groups=mesh['seq'=8,'dp'=4] {'seq'}, dimensions={0} | all-to-all | bytes 3276800 | tf_op jit(solution)/shard_map/all_to_all | solution.py:94
  163.6 53.9 %fusion = f32[24,5120]{1,0:T(8,128)S(1)} fusion(f32[80,5120]{1,0:T(8,128)S(1)} %bitcast.101), kind=kCustom, calls=%all-reduce-scatter | all-reduce-scatter fusion | flops 491521 | bytes 2130432
  217.5 1.3 collective-permute-start
  218.8 0.6 dynamic-slice.5
  220.1 5.0 %collective-permute-done = f32[12,5120]{1,0:T(8,128)S(1)} collective-permute-done((f32[12,5120]{1,0:T(8,128)S(1)}, f32[12,5120]{1,0:T(8,128)S(1)}, u32[]{:S(2)}, u32[]{:S(2)}) %collective-permute-start) | collective-permute-done | bytes 245792
  225.6 0.8 constant_dynamic-slice_fusion
  (30 shorter events, 3.1 us)
Async XLA Ops:
  7.2 65.8 %reduce-scatter.7.cloned.1.call-start = ((), (), s32[]{:S(2)}) async-start(), calls=%async_computation.5 | async-start | bytes 1179648 | tf_op jit(solution)/shard_map/reduce_scatter | solution.py:74
  7.2 5.7 %copy-start = (bf16[1,128,5120]{2,1,0:T(8,128)(2,1)S(1)}, bf16[1,128,5120]{2,1,0:T(8,128)(2,1)}, u32[]{:S(2)}) copy-start(bf16[1,128,5120]{2,1,0:T(8,128)(2,1)} %param.7) | copy-start | bytes 3932164
  12.9 4.3 %copy-start.3 = (bf16[5120,128]{1,0:T(8,128)(2,1)S(1)}, bf16[5120,128]{1,0:T(8,128)(2,1)}, u32[]{:S(2)}) copy-start(bf16[5120,128]{1,0:T(8,128)(2,1)} %param.11) | copy-start | bytes 3932164
  37.1 71.3 %all-gather.3.cloned.1.call-start = ((), (), s32[]{:S(2)}) async-start(), calls=%async_computation.6 | async-start | bytes 2064384 | tf_op jit(solution)/shard_map/all_gather | solution.py:85
  74.6 62.0 %all-gather.5.cloned.1.call-start = ((), (), s32[]{:S(2)}) async-start(), calls=%async_computation.7 | async-start | bytes 1474560 | tf_op jit(solution)/shard_map/all_gather | solution.py:86
  76.8 4.4 %copy-start.1 = (bf16[1,128,5120]{2,1,0:T(8,128)(2,1)S(1)}, bf16[1,128,5120]{2,1,0:T(8,128)(2,1)}, u32[]{:S(2)}) copy-start(bf16[1,128,5120]{2,1,0:T(8,128)(2,1)} %param.8) | copy-start | bytes 3932164
  76.8 21.5 %all-to-all-start = ((bf16[128,8,640]{0,2,1:T(8,128)(2,1)}), bf16[128,8,640]{0,2,1:T(8,128)(2,1)S(1)}, u32[]{:S(2)}, u32[]{:S(2)}) async-start(bf16[128,8,640]{0,2,1:T(8,128)(2,1)} %bitcast.23), calls=%async_computation.1 | async-start | bytes 2621440 | tf_op jit(solution)/shard_map/all_to_all | solution.py:81
  98.4 24.2 %all-to-all-start.1 = ((bf16[128,8,640]{2,0,1:T(8,128)(2,1)}), bf16[128,8,640]{2,0,1:T(8,128)(2,1)}, u32[]{:S(2)}, u32[]{:S(2)}) async-start(bf16[128,8,640]{2,0,1:T(8,128)(2,1)} %copy.55), calls=%async_computation.2 | async-start | bytes 2621440 | tf_op jit(solution)/shard_map/all_to_all | solution.py:82
  106.1 120.4 %reduce-scatter.9.cloned.1.call-start = ((), (), s32[]{:S(2)}) async-start(), calls=%async_computation.8 | async-start | bytes 2867200
  163.6 55.2 %copy-start.2 = (u32[32]{0:T(128)S(1)}, u32[32]{0:T(128)}, u32[]{:S(2)}) copy-start(u32[32]{0:T(128)} %constant.62) | copy-start | bytes 388
  217.5 7.6 %collective-permute-start = (f32[12,5120]{1,0:T(8,128)S(1)}, f32[12,5120]{1,0:T(8,128)S(1)}, u32[]{:S(2)}, u32[]{:S(2)}) collective-permute-start(f32[12,5120]{1,0:T(8,128)S(1)} %slice.10), channel_id=1, source_target_pairs={{0,1},{1,2},{2,3},{4,5},{5,6},{6,7},{8,9},{9,10},{10,11},{12,13},{... | collective-permute-start | bytes 737288
Sparse Core Ops, SparseCore 0:
  37.2 35.7 reduce-scatter.6
  75.5 32.9 all-gather.2
  110.3 26.2 all-gather.4
  139.4 57.8 reduce-scatter.8
where the time goes:
time: 235 us; the launch traced here: 233 us
  blocking collectives  89.2 us (38%)
  waiting for transfers between devices  80.4 us (34%)
  matrix products  22.2 us (9%)
  between operations  14.6 us (6%)
  starting transfers between devices  13.5 us (6%)
  local copies, waits for them, and re-layouts  8.92 us (4%)
  other arithmetic  4.09 us (2%)
    unnamed x1, blocking collectives  53.9 us
    reduce_scatter x1, waiting for transfers between devices, shards(): lax.psum_scatter(jnp.concatenate([key_term, value_term], axis=1), 'seq',...  35.4 us
    all_to_all x1, blocking collectives, shards(): lax.all_to_all(out_cols, 'seq', split_axis=0, concat_axis=1, tiled=True)  23.9 us
    all_to_all x1, waiting for transfers between devices, shards(): lax.all_to_all(inputs_row, 'seq', split_axis=1, concat_axis=0, tiled=True)  15.7 us
    all_gather x1, waiting for transfers between devices, shards(): lax.all_gather(attn_flat, 'seq', axis=0, tiled=True)  14.1 us
    all_gather x1, blocking collectives, shards(): kv_all = lax.all_gather(kv_local, 'seq', axis=0, tiled=True)  11.4 us
    all_to_all x1, waiting for transfers between devices, shards(): lax.all_to_all(grad_row, 'seq', split_axis=1, concat_axis=0, tiled=True)  8.52 us
    all_to_all x1, starting transfers between devices, shards(): lax.all_to_all(grad_row, 'seq', split_axis=1, concat_axis=0, tiled=True)  7.72 us
  transfers between devices with their start and end apart: 7, of which 6 were waited for; matrix products, arithmetic and copies ran while one was open for 30% of the time, Pallas kernels for 0%

commit v1 on v0

v1 whole, which is shorter than its diff:
```python
import functools
import math

import jax
import jax.numpy as jnp
import ml_dtypes
import numpy as np
from jax import lax
from jax.experimental import pallas as pl
from jax.experimental.pallas import tpu as pltpu
from jax.sharding import PartitionSpec as P

F32 = jnp.float32
BF16 = jnp.bfloat16
MESH = pl.DeviceIdType.MESH
NT = (((1,), (1,)), ((), ()))
TN = (((0,), (0,)), ((), ()))


def round_up(value, step):
    return -(-value // step) * step


def head_row_selection(n_seq, n_dp, width):
    rows = width // (n_seq * n_dp)
    padded = round_up(rows, 8)
    chips = n_seq // 2
    table = np.zeros((width, 2, n_dp, chips, padded), np.float32)
    for core in range(2):
        for d in range(n_dp):
            for c in range(chips):
                for i in range(rows):
                    table[((c * 2 + core) * n_dp + d) * rows + i, core, d, c, i] = 1.0
    return table.reshape(width, -1).astype(ml_dtypes.bfloat16)


def kernel(
    n_seq, n_dp,
    x_ref, og_ref, wq_hbm, wk_hbm, wv_hbm, wo_hbm, mask_ref, sel_hbm,
    oqkv_ref, oout_ref,
    wq, wkv, wo, sel, xbuf, gbuf, kvall, kvsend, kvrecv, kvacc, abuf, qbuf, kgbuf,
    q3, d3, dt3, a3, qg3, kt, vt, bias,
    part_o, part_q, part_k,
    exo_s, exo_r, exq_s, exq_r, exk_s, exk_r,
    dpo_s, dpo_r, dpq_s, dpq_r, dpk_s, dpk_r, fo_s, fo_r,
    wsem, s_x, r_x, s_g, r_g, s_kv, r_kv, s_kr, r_kr, s_a, r_a, s_q, r_q, s_kg, r_kg,
    s_ex, r_ex, s_do, r_do, s_dq, r_dq, s_dk, r_dk, s_fo, r_fo,
):
    chips = n_seq // 2
    me = lax.axis_index("seq")
    md = lax.axis_index("dp")
    core = lax.rem(me, 2)
    chip = lax.div(me, 2)
    other = 1 - core
    tokens, depth = x_ref.shape
    heads, _, head = q3.shape
    width = depth // chips
    half = width // 2
    length = n_seq * tokens
    scale = 1.0 / math.sqrt(head)

    loads = [
        pltpu.make_async_copy(wk_hbm, wkv.at[:, 0:head], wsem.at[0]),
        pltpu.make_async_copy(wv_hbm, wkv.at[:, head : 2 * head], wsem.at[1]),
        pltpu.make_async_copy(wq_hbm, wq, wsem.at[2]),
        pltpu.make_async_copy(wo_hbm, wo, wsem.at[3]),
        pltpu.make_async_copy(sel_hbm, sel, wsem.at[4]),
    ]
    for load in loads:
        load.start()

    barrier = pltpu.get_barrier_semaphore()
    for k in range(1, n_seq):
        pl.semaphore_signal(
            barrier, inc=1, device_id={"seq": lax.rem(me + k, n_seq)}, device_id_type=MESH
        )
    for k in range(1, n_dp):
        pl.semaphore_signal(
            barrier, inc=1, device_id={"dp": lax.rem(md + k, n_dp)}, device_id_type=MESH
        )
    pl.semaphore_wait(barrier, n_seq + n_dp - 2)

    sent = []

    def spread(source, dest, slot, index, count, to_device, send_sems, recv_sems):
        copies = []
        for k in range(1, count):
            peer = lax.rem(index + k, count)
            copy = pltpu.make_async_remote_copy(
                src_ref=source(peer),
                dst_ref=dest.at[slot],
                send_sem=send_sems.at[k - 1],
                recv_sem=recv_sems.at[k - 1],
                device_id=to_device(peer),
                device_id_type=MESH,
            )
            copy.start()
            copies.append(copy)
        sent.extend(copies)
        return copies

    def to_seq(peer):
        return {"seq": peer}

    def to_chip(peer):
        return {"seq": peer * 2 + core}

    def to_dp(peer):
        return {"dp": peer}

    def over_chips(buf, send_sems, recv_sems):
        return spread(
            lambda peer: buf.at[chip], buf, chip, chip, chips, to_chip, send_sems, recv_sems
        )

    def swap(source, dest, i):
        copy = pltpu.make_async_remote_copy(
            src_ref=source, dst_ref=dest, send_sem=s_ex.at[i], recv_sem=r_ex.at[i],
            device_id={"seq": chip * 2 + other}, device_id_type=MESH,
        )
        copy.start()
        sent.append(copy)
        return copy

    def arrive(copies):
        for copy in copies:
            copy.wait_recv()

    def columns(index):
        return pl.ds(pl.multiple_of(index * width, 128), width)

    loads[0].wait()
    loads[1].wait()
    kvall[me] = jnp.dot(x_ref[...], wkv[...], preferred_element_type=F32).astype(BF16)
    got_kv = spread(lambda peer: kvall.at[me], kvall, me, me, n_seq, to_seq, s_kv, r_kv)

    got_g = spread(
        lambda peer: og_ref.at[:, columns(peer)], gbuf, chip, chip, chips, to_chip, s_g, r_g
    )
    got_x = spread(
        lambda peer: x_ref.at[:, columns(peer)], xbuf, chip, chip, chips, to_chip, s_x, r_x
    )
    xbuf[chip] = x_ref[:, columns(chip)]
    gbuf[chip] = og_ref[:, columns(chip)]

    loads[2].wait()
    queries = jnp.dot(x_ref[...], wq[...], preferred_element_type=F32)
    for g in range(heads):
        q3[g] = queries[:, g * head : (g + 1) * head].astype(BF16)
    loads[3].wait()
    for g in range(heads):
        grad_t = lax.dot_general(
            wo[g * head : (g + 1) * head, :], og_ref[...], NT, preferred_element_type=F32
        )
        dt3[g] = grad_t.astype(BF16)
        d3[g] = grad_t.T.astype(BF16)

    gap = lax.broadcasted_iota(jnp.int32, (tokens, tokens), 0) - lax.broadcasted_iota(
        jnp.int32, (tokens, tokens), 1
    )
    for j in range(n_seq):
        reach = jnp.where(mask_ref[me, j] == 1, jnp.where(me == j, 0, 4 * tokens), -4 * tokens)
        bias[j * tokens : (j + 1) * tokens, :] = jnp.where(gap <= reach, 0.0, -jnp.inf)

    kvacc[...] = jnp.zeros_like(kvacc)
    arrive(got_kv)
    for j in range(n_seq):
        rows = slice(j * tokens, (j + 1) * tokens)
        kt[:, rows] = kvall[j, :, 0:head].astype(F32).T.astype(BF16)
        vt[:, rows] = kvall[j, :, head : 2 * head].astype(F32).T.astype(BF16)

    @pl.loop(0, heads)
    def _(g):
        keys = kvall[:, :, 0:head].reshape(length, head)
        values = kvall[:, :, head : 2 * head].reshape(length, head)
        query = q3[g]
        grad_t = dt3[g]
        scores = lax.dot_general(keys, query, NT, preferred_element_type=F32) * scale + bias[...]
        top = jnp.max(scores, axis=0, keepdims=True)
        raised = jnp.exp(scores - top)
        probs = raised * (1.0 / jnp.sum(raised, axis=0, keepdims=True))
        weights = probs.astype(BF16)
        out_t = jnp.dot(vt[...], weights, preferred_element_type=F32).astype(BF16).astype(F32)
        delta = jnp.sum(grad_t.astype(F32) * out_t, axis=0, keepdims=True)
        prob_grad = jnp.dot(values, grad_t, preferred_element_type=F32)
        score_grad = (probs * (prob_grad - delta)).astype(BF16)
        a3[g] = out_t.T.astype(BF16)
        query_t = jnp.dot(kt[...], score_grad, preferred_element_type=F32) * scale
        qg3[g] = query_t.T.astype(BF16)
        kvacc[:, 0:head] += jnp.dot(score_grad, query, preferred_element_type=F32)
        kvacc[:, head : 2 * head] += jnp.dot(weights, d3[g], preferred_element_type=F32)

    loads[4].wait()
    attn = jnp.concatenate([a3[g] for g in range(heads)], axis=1)
    abuf[chip] = jnp.dot(attn, sel[...], preferred_element_type=F32).astype(BF16)
    got_a = over_chips(abuf, s_a, r_a)
    for j in range(n_seq):
        rows = slice(j * tokens, (j + 1) * tokens)
        kvsend[j, :, 0:head] = (kvacc[rows, 0:head] * scale).astype(BF16)
        kvsend[j, :, head : 2 * head] = kvacc[rows, head : 2 * head].astype(BF16)
    got_kr = spread(lambda peer: kvsend.at[peer], kvrecv, me, me, n_seq, to_seq, s_kr, r_kr)
    for g in range(heads):
        qbuf[chip, :, g * head : (g + 1) * head] = qg3[g]
    got_q = over_chips(qbuf, s_q, r_q)

    arrive(got_g)
    arrive(got_a)
    group = exo_s.shape[1]
    side = n_dp * group
    grads = gbuf[...].reshape(chips * tokens, width)

    def out_rows(which):
        picked = abuf[:, :, pl.ds(pl.multiple_of(which * side, 128), side)]
        return lax.dot_general(
            picked.reshape(chips * tokens, side), grads, TN, preferred_element_type=F32
        )

    theirs = out_rows(other)
    for d in range(n_dp):
        exo_s[d] = theirs[d * group : (d + 1) * group, :].astype(BF16)
    got_exo = swap(exo_s, exo_r, 0)
    part_o[...] = out_rows(core)

    arrive(got_kr)
    own = pl.ds(pl.multiple_of(me * tokens, tokens), tokens)
    key_sum = kvacc[own, 0:head] * scale
    value_sum = kvacc[own, head : 2 * head]
    for k in range(1, n_seq):
        peer = lax.rem(me + k, n_seq)
        key_sum += kvrecv[peer, :, 0:head].astype(F32)
        value_sum += kvrecv[peer, :, head : 2 * head].astype(F32)
    kgbuf[chip, :, 0:head] = key_sum.astype(BF16)
    kgbuf[chip, :, head : 2 * head] = value_sum.astype(BF16)
    got_kg = over_chips(kgbuf, s_kg, r_kg)

    got_exo.wait_recv()
    for d in range(n_dp):
        dpo_s[d] = (part_o[d * group : (d + 1) * group, :] + exo_r[d].astype(F32)).astype(BF16)
    got_do = spread(lambda peer: dpo_s.at[peer], dpo_r, md, md, n_dp, to_dp, s_do, r_do)

    owned = exq_s.shape[1]

    def rows_of(which, d):
        return pl.ds(pl.multiple_of(which * half + d * owned, 8), owned)

    def projection(grad_buf, part, ex_s, ex_r, i):
        features = xbuf[...].reshape(chips * tokens, width)
        grad = grad_buf[...].reshape(chips * tokens, grad_buf.shape[2])
        part[...] = lax.dot_general(features, grad, TN, preferred_element_type=F32)
        for d in range(n_dp):
            ex_s[d] = part[rows_of(other, d), :].astype(BF16)
        return swap(ex_s, ex_r, i)

    def reduce_dp(got_ex, part, ex_r, dp_s, dp_r, send_sems, recv_sems):
        got_ex.wait_recv()
        for d in range(n_dp):
            dp_s[d] = (part[rows_of(core, d), :] + ex_r[d].astype(F32)).astype(BF16)
        return spread(lambda peer: dp_s.at[peer], dp_r, md, md, n_dp, to_dp, send_sems, recv_sems)

    arrive(got_x)
    arrive(got_q)
    got_exq = projection(qbuf, part_q, exq_s, exq_r, 1)
    arrive(got_kg)
    got_dq = reduce_dp(got_exq, part_q, exq_r, dpq_s, dpq_r, s_dq, r_dq)
    got_exk = projection(kgbuf, part_k, exk_s, exk_r, 2)
    got_dk = reduce_dp(got_exk, part_k, exk_r, dpk_s, dpk_r, s_dk, r_dk)

    arrive(got_do)
    mine = pl.ds(pl.multiple_of(md * group, 8), group)
    total = part_o[mine, :] + exo_r[md].astype(F32)
    for k in range(1, n_dp):
        total += dpo_r[lax.rem(md + k, n_dp)].astype(F32)
    padded = group // chips
    for c in range(chips):
        fo_s[c] = total[c * padded : (c + 1) * padded, :].astype(BF16)
    got_fo = spread(lambda peer: fo_s.at[peer], fo_r, chip, chip, chips, to_chip, s_fo, r_fo)
    fo_r[chip] = fo_s[chip]

    def finish(part, ex_r, dp_r):
        result = part[rows_of(core, md), :] + ex_r[md].astype(F32)
        for k in range(1, n_dp):
            result += dp_r[lax.rem(md + k, n_dp)].astype(F32)
        return result

    q_columns = heads * head
    arrive(got_dq)
    oqkv_ref[:, 0:q_columns] = finish(part_q, exq_r, dpq_r)
    arrive(got_dk)
    oqkv_ref[:, q_columns:] = finish(part_k, exk_r, dpk_r)
    arrive(got_fo)
    for c in range(chips):
        oout_ref[:, c * width : (c + 1) * width] = fo_r[c].astype(F32)[0 : oout_ref.shape[0], :]
    for copy in sent:
        copy.wait_send()


def shards(n_seq, n_dp, layer_input, out_grad, w_query, w_key, w_value, w_output, block_mask):
    tokens, depth = layer_input.shape[1:]
    head = w_key.shape[1]
    q_width = w_query.shape[1]
    heads = q_width // head
    chips = n_seq // 2
    devices = n_seq * n_dp
    width = depth // chips
    rows_in = depth // devices
    rows_out = q_width // devices
    group = chips * round_up(rows_out, 8)
    side = n_dp * group
    length = n_seq * tokens
    selection = jnp.asarray(head_row_selection(n_seq, n_dp, q_width))
    vmem = pltpu.VMEM
    scratch = [
        vmem((depth, q_width), BF16), vmem((depth, 2 * head), BF16), vmem((q_width, depth), BF16),
        vmem((q_width, 2 * side), BF16),
        vmem((chips, tokens, width), BF16), vmem((chips, tokens, width), BF16),
        vmem((n_seq, tokens, 2 * head), BF16), vmem((n_seq, tokens, 2 * head), BF16),
        vmem((n_seq, tokens, 2 * head), BF16), vmem((length, 2 * head), F32),
        vmem((chips, tokens, 2 * side), BF16), vmem((chips, tokens, q_width), BF16),
        vmem((chips, tokens, 2 * head), BF16),
    ]
    scratch += [vmem((heads, tokens, head), BF16)] * 2 + [vmem((heads, head, tokens), BF16)]
    scratch += [vmem((heads, tokens, head), BF16)] * 2
    scratch += [vmem((head, length), BF16)] * 2 + [vmem((length, tokens), F32)]
    scratch += [vmem((side, width), F32), vmem((width, q_width), F32), vmem((width, 2 * head), F32)]
    out_block = vmem((n_dp, group, width), BF16)
    q_block = vmem((n_dp, rows_in, q_width), BF16)
    k_block = vmem((n_dp, rows_in, 2 * head), BF16)
    scratch += [out_block] * 2 + [q_block] * 2 + [k_block] * 2
    scratch += [out_block] * 2 + [q_block] * 2 + [k_block] * 2
    scratch += [vmem((chips, group // chips, width), BF16)] * 2
    dma = pltpu.SemaphoreType.DMA
    sems = [dma((5,))]
    for count in (chips, chips, n_seq, n_seq, chips, chips, chips, 4, n_dp, n_dp, n_dp, chips):
        sems += [dma((count - 1,))] * 2
    in_vmem = pl.BlockSpec(memory_space=pltpu.VMEM)
    in_hbm = pl.BlockSpec(memory_space=pl.ANY)
    return pl.pallas_call(
        functools.partial(kernel, n_seq, n_dp),
        out_shape=(
            jax.ShapeDtypeStruct((rows_in, q_width + 2 * head), F32),
            jax.ShapeDtypeStruct((rows_out, depth), F32),
        ),
        in_specs=[in_vmem, in_vmem, in_hbm, in_hbm, in_hbm, in_hbm,
                  pl.BlockSpec(memory_space=pltpu.SMEM), in_hbm],
        out_specs=(in_vmem, in_vmem),
        scratch_shapes=scratch + sems,
        compiler_params=pltpu.CompilerParams(
            collective_id=0, has_side_effects=True, vmem_limit_bytes=60 * 1024 * 1024
        ),
    )(layer_input[0], out_grad[0], w_query, w_key, w_value, w_output, block_mask[0], selection)


def solution(mesh):
    placed = (P("dp", "seq", None), P("dp", "seq", None), P(), P(), P(), P(), P("dp", None, None))
    return jax.shard_map(
        functools.partial(shards, mesh.shape["seq"], mesh.shape["dp"]),
        mesh=mesh,
        in_specs=placed,
        out_specs=(P(("seq", "dp"), None), P(("seq", "dp"), None)),
        check_vma=False,
    )
```

time: 235 us -> 109 us (0.46)
  Pallas kernels: 0 us -> 105 us
  blocking collectives: 89.2 us -> 0 us
  waiting for transfers between devices: 80.4 us -> 0 us
  matrix products: 22.2 us -> 0 us
  between operations: 14.6 us -> 0.65 us
  starting transfers between devices: 13.5 us -> 0 us
  local copies, waits for them, and re-layouts: 8.92 us -> 2.74 us
  other arithmetic: 4.09 us -> 0 us
    pallas_call x0 -> x1, Pallas kernels: none -> 105 us  [shards(): pl.pallas_call(functools.partial(kernel, n_seq, n_dp), out_shape=(jax.Sha...]
    unnamed x1 -> x0, blocking collectives: 53.9 us -> none
    reduce_scatter x1 -> x0, waiting for transfers between devices: 35.4 us -> none  [shards(): lax.psum_scatter(jnp.concatenate([key_term, value_term], axis=1), 'seq',...]
    all_to_all x2 -> x0, waiting for transfers between devices: 24.2 us -> none  [the longest x1 15.7 us: shards(): lax.all_to_all(inputs_row, 'seq', split_axis=1, concat_axis=0, tiled=True)]
    all_to_all x1 -> x0, blocking collectives: 23.9 us -> none  [shards(): lax.all_to_all(out_cols, 'seq', split_axis=0, concat_axis=1, tiled=True)]
    dot_general x11 -> x0, matrix products: 22.2 us -> none  [the longest x1 5.48 us: shards(): lax.dot_general(grad_row, w_output, (((1,), (1,)), ((), ())), preferred_e...]
    all_gather x2 -> x0, waiting for transfers between devices: 15 us -> none  [the longest x1 14.1 us: shards(): lax.all_gather(attn_flat, 'seq', axis=0, tiled=True)]
    all_to_all x2 -> x0, starting transfers between devices: 12.1 us -> none  [the longest x1 7.72 us: shards(): lax.all_to_all(grad_row, 'seq', split_axis=1, concat_axis=0, tiled=True)]
  transfers between devices with their start and end apart: 7 -> 0, of which waited for: 6 -> 0; matrix products, arithmetic and copies ran while one was open for 30% -> 0% of each run, Pallas kernels for 0% -> 0%
where the time goes in v1:
time: 109 us
  Pallas kernels  105 us (96%)
  local copies, waits for them, and re-layouts  2.74 us (3%)
    pallas_call x1, Pallas kernels, shards(): pl.pallas_call(functools.partial(kernel, n_seq, n_dp), out_shape=(jax.Sha...  105 us
    unnamed x4, local copies, waits for them, and re-layouts  2.74 us

profile of v1, /device:TPU:1, one launch (start us, length us, event | category | flops | bytes accessed | tf_op | source)
XLA Modules:
  0.0 108.9 jit_solution(5102312940401421543)
XLA Ops:
  0.6 105.5 %shard_map.95 = (f32[160,896]{1,0:T(8,128)}, f32[20,5120]{1,0:T(8,128)}) custom-call(bf16[128,5120]{1,0:T(8,128)(2,1)} %bitcast.3, bf16[128,5120]{1,0:T(8,128)(2,1)} %bitcast.4, bf16[5120,640]{1,0:T(8,128)(2,1)} %wq_hbm.1, bf16[5120,128]{1,0:T(8,128)(2,1)} %wk_hbm.1, bf16[5120,128]{1,0:T(8,128)(2,1)} %wv_hbm.1, bf16[640,5120]{1,0:T(8,128)(2,1)} %wo_hbm.1, ...), custom_call_target="tpu_custom_call" | custom-call | tf_op jit(solution)/shard_map/pallas_call | solution.py:337
  106.1 0.0 copy-start
  106.1 2.0 %copy.12 = f32[160,896]{1,0:T(8,128)} copy(f32[160,896]{1,0:T(8,128)} %get-tuple-element.4) | data formatting | bytes 1146880
  108.1 0.0 copy-done
  108.1 0.8 copy.13
Async XLA Ops:
  106.1 2.0 %copy-start = (f32[20,5120]{1,0:T(8,128)S(1)}, f32[20,5120]{1,0:T(8,128)}, u32[]{:S(2)}) copy-start(f32[20,5120]{1,0:T(8,128)} %get-tuple-element.5) | copy-start | bytes 1228804

commit v2 on v1

--- a/solution.py
+++ b/solution.py
@@ -36,9 +36,9 @@
 
 def kernel(
     n_seq, n_dp,
-    x_ref, og_ref, wq_hbm, wk_hbm, wv_hbm, wo_hbm, mask_ref, sel_hbm,
+    x_hbm, og_hbm, wq_hbm, wk_hbm, wv_hbm, wo_hbm, mask_ref, sel_hbm,
     oqkv_ref, oout_ref,
-    wq, wkv, wo, sel, xbuf, gbuf, kvall, kvsend, kvrecv, kvacc, abuf, qbuf, kgbuf,
+    x_ref, og_ref, wq, wkv, wo, sel, xbuf, gbuf, kvall, kvsend, kvrecv, kvacc, abuf, qbuf, kgbuf,
     q3, d3, dt3, a3, qg3, kt, vt, bias,
     part_o, part_q, part_k,
     exo_s, exo_r, exq_s, exq_r, exk_s, exk_r,
@@ -62,6 +62,8 @@
     loads = [
         pltpu.make_async_copy(wk_hbm, wkv.at[:, 0:head], wsem.at[0]),
         pltpu.make_async_copy(wv_hbm, wkv.at[:, head : 2 * head], wsem.at[1]),
+        pltpu.make_async_copy(x_hbm, x_ref, wsem.at[5]),
+        pltpu.make_async_copy(og_hbm, og_ref, wsem.at[6]),
         pltpu.make_async_copy(wq_hbm, wq, wsem.at[2]),
         pltpu.make_async_copy(wo_hbm, wo, wsem.at[3]),
         pltpu.make_async_copy(sel_hbm, sel, wsem.at[4]),
@@ -129,25 +131,25 @@
     def columns(index):
         return pl.ds(pl.multiple_of(index * width, 128), width)
 
+    got_g = spread(
+        lambda peer: og_hbm.at[:, columns(peer)], gbuf, chip, chip, chips, to_chip, s_g, r_g
+    )
+
     loads[0].wait()
     loads[1].wait()
+    loads[2].wait()
     kvall[me] = jnp.dot(x_ref[...], wkv[...], preferred_element_type=F32).astype(BF16)
     got_kv = spread(lambda peer: kvall.at[me], kvall, me, me, n_seq, to_seq, s_kv, r_kv)
 
-    got_g = spread(
-        lambda peer: og_ref.at[:, columns(peer)], gbuf, chip, chip, chips, to_chip, s_g, r_g
-    )
-    got_x = spread(
-        lambda peer: x_ref.at[:, columns(peer)], xbuf, chip, chip, chips, to_chip, s_x, r_x
-    )
+    loads[3].wait()
     xbuf[chip] = x_ref[:, columns(chip)]
     gbuf[chip] = og_ref[:, columns(chip)]
 
-    loads[2].wait()
+    loads[4].wait()
     queries = jnp.dot(x_ref[...], wq[...], preferred_element_type=F32)
     for g in range(heads):
         q3[g] = queries[:, g * head : (g + 1) * head].astype(BF16)
-    loads[3].wait()
+    loads[5].wait()
     for g in range(heads):
         grad_t = lax.dot_general(
             wo[g * head : (g + 1) * head, :], og_ref[...], NT, preferred_element_type=F32
@@ -190,7 +192,7 @@
         kvacc[:, 0:head] += jnp.dot(score_grad, query, preferred_element_type=F32)
         kvacc[:, head : 2 * head] += jnp.dot(weights, d3[g], preferred_element_type=F32)
 
-    loads[4].wait()
+    loads[6].wait()
     attn = jnp.concatenate([a3[g] for g in range(heads)], axis=1)
     abuf[chip] = jnp.dot(attn, sel[...], preferred_element_type=F32).astype(BF16)
     got_a = over_chips(abuf, s_a, r_a)
@@ -198,13 +200,16 @@
         rows = slice(j * tokens, (j + 1) * tokens)
         kvsend[j, :, 0:head] = (kvacc[rows, 0:head] * scale).astype(BF16)
         kvsend[j, :, head : 2 * head] = kvacc[rows, head : 2 * head].astype(BF16)
-    got_kr = spread(lambda peer: kvsend.at[peer], kvrecv, me, me, n_seq, to_seq, s_kr, r_kr)
     for g in range(heads):
         qbuf[chip, :, g * head : (g + 1) * head] = qg3[g]
-    got_q = over_chips(qbuf, s_q, r_q)
 
     arrive(got_g)
     arrive(got_a)
+    got_kr = spread(lambda peer: kvsend.at[peer], kvrecv, me, me, n_seq, to_seq, s_kr, r_kr)
+    got_x = spread(
+        lambda peer: x_hbm.at[:, columns(peer)], xbuf, chip, chip, chips, to_chip, s_x, r_x
+    )
+    got_q = over_chips(qbuf, s_q, r_q)
     group = exo_s.shape[1]
     side = n_dp * group
     grads = gbuf[...].reshape(chips * tokens, width)
@@ -220,6 +225,11 @@
         exo_s[d] = theirs[d * group : (d + 1) * group, :].astype(BF16)
     got_exo = swap(exo_s, exo_r, 0)
     part_o[...] = out_rows(core)
+
+    got_exo.wait_recv()
+    for d in range(n_dp):
+        dpo_s[d] = (part_o[d * group : (d + 1) * group, :] + exo_r[d].astype(F32)).astype(BF16)
+    got_do = spread(lambda peer: dpo_s.at[peer], dpo_r, md, md, n_dp, to_dp, s_do, r_do)
 
     arrive(got_kr)
     own = pl.ds(pl.multiple_of(me * tokens, tokens), tokens)
@@ -233,11 +243,6 @@
     kgbuf[chip, :, head : 2 * head] = value_sum.astype(BF16)
     got_kg = over_chips(kgbuf, s_kg, r_kg)
 
-    got_exo.wait_recv()
-    for d in range(n_dp):
-        dpo_s[d] = (part_o[d * group : (d + 1) * group, :] + exo_r[d].astype(F32)).astype(BF16)
-    got_do = spread(lambda peer: dpo_s.at[peer], dpo_r, md, md, n_dp, to_dp, s_do, r_do)
-
     owned = exq_s.shape[1]
 
     def rows_of(which, d):
@@ -260,10 +265,7 @@
     arrive(got_x)
     arrive(got_q)
     got_exq = projection(qbuf, part_q, exq_s, exq_r, 1)
-    arrive(got_kg)
     got_dq = reduce_dp(got_exq, part_q, exq_r, dpq_s, dpq_r, s_dq, r_dq)
-    got_exk = projection(kgbuf, part_k, exk_s, exk_r, 2)
-    got_dk = reduce_dp(got_exk, part_k, exk_r, dpk_s, dpk_r, s_dk, r_dk)
 
     arrive(got_do)
     mine = pl.ds(pl.multiple_of(md * group, 8), group)
@@ -275,6 +277,10 @@
         fo_s[c] = total[c * padded : (c + 1) * padded, :].astype(BF16)
     got_fo = spread(lambda peer: fo_s.at[peer], fo_r, chip, chip, chips, to_chip, s_fo, r_fo)
     fo_r[chip] = fo_s[chip]
+
+    arrive(got_kg)
+    got_exk = projection(kgbuf, part_k, exk_s, exk_r, 2)
+    got_dk = reduce_dp(got_exk, part_k, exk_r, dpk_s, dpk_r, s_dk, r_dk)
 
     def finish(part, ex_r, dp_r):
         result = part[rows_of(core, md), :] + ex_r[md].astype(F32)
@@ -310,6 +316,7 @@
     selection = jnp.asarray(head_row_selection(n_seq, n_dp, q_width))
     vmem = pltpu.VMEM
     scratch = [
+        vmem((tokens, depth), BF16), vmem((tokens, depth), BF16),
         vmem((depth, q_width), BF16), vmem((depth, 2 * head), BF16), vmem((q_width, depth), BF16),
         vmem((q_width, 2 * side), BF16),
         vmem((chips, tokens, width), BF16), vmem((chips, tokens, width), BF16),
@@ -329,7 +336,7 @@
     scratch += [out_block] * 2 + [q_block] * 2 + [k_block] * 2
     scratch += [vmem((chips, group // chips, width), BF16)] * 2
     dma = pltpu.SemaphoreType.DMA
-    sems = [dma((5,))]
+    sems = [dma((7,))]
     for count in (chips, chips, n_seq, n_seq, chips, chips, chips, 4, n_dp, n_dp, n_dp, chips):
         sems += [dma((count - 1,))] * 2
     in_vmem = pl.BlockSpec(memory_space=pltpu.VMEM)
@@ -340,7 +347,7 @@
             jax.ShapeDtypeStruct((rows_in, q_width + 2 * head), F32),
             jax.ShapeDtypeStruct((rows_out, depth), F32),
         ),
-        in_specs=[in_vmem, in_vmem, in_hbm, in_hbm, in_hbm, in_hbm,
+        in_specs=[in_hbm, in_hbm, in_hbm, in_hbm, in_hbm, in_hbm,
                   pl.BlockSpec(memory_space=pltpu.SMEM), in_hbm],
         out_specs=(in_vmem, in_vmem),
         scratch_shapes=scratch + sems,

time: 109 us -> 108 us (level)
  no operation moved by 1% of the time
where the time goes in v2:
time: 108 us
  Pallas kernels  105 us (97%)
  local copies, waits for them, and re-layouts  2.74 us (3%)
    pallas_call x1, Pallas kernels, shards(): pl.pallas_call(functools.partial(kernel, n_seq, n_dp), out_shape=(jax.Sha...  105 us
    unnamed x4, local copies, waits for them, and re-layouts  2.74 us

profile of v2, /device:TPU:1, one launch (start us, length us, event | category | flops | bytes accessed | tf_op | source)
XLA Modules:
  0.0 108.0 jit_solution(1969194610288885315)
XLA Ops:
  0.6 104.6 %shard_map.95 = (f32[160,896]{1,0:T(8,128)}, f32[20,5120]{1,0:T(8,128)}) custom-call(bf16[128,5120]{1,0:T(8,128)(2,1)} %bitcast.3, bf16[128,5120]{1,0:T(8,128)(2,1)} %bitcast.4, bf16[5120,640]{1,0:T(8,128)(2,1)} %wq_hbm.1, bf16[5120,128]{1,0:T(8,128)(2,1)} %wk_hbm.1, bf16[5120,128]{1,0:T(8,128)(2,1)} %wv_hbm.1, bf16[640,5120]{1,0:T(8,128)(2,1)} %wo_hbm.1, ...), custom_call_target="tpu_custom_call" | custom-call | tf_op jit(solution)/shard_map/pallas_call | solution.py:344
  105.3 0.0 copy-start
  105.3 2.0 %copy.12 = f32[160,896]{1,0:T(8,128)} copy(f32[160,896]{1,0:T(8,128)} %get-tuple-element.4) | data formatting | bytes 1146880
  107.2 0.0 copy-done
  107.2 0.8 copy.13
Async XLA Ops:
  105.3 2.0 %copy-start = (f32[20,5120]{1,0:T(8,128)S(1)}, f32[20,5120]{1,0:T(8,128)}, u32[]{:S(2)}) copy-start(f32[20,5120]{1,0:T(8,128)} %get-tuple-element.5) | copy-start | bytes 1228804

commit v3 on v2

--- a/solution.py
+++ b/solution.py
@@ -38,7 +38,7 @@
     n_seq, n_dp,
     x_hbm, og_hbm, wq_hbm, wk_hbm, wv_hbm, wo_hbm, mask_ref, sel_hbm,
     oqkv_ref, oout_ref,
-    x_ref, og_ref, wq, wkv, wo, sel, xbuf, gbuf, kvall, kvsend, kvrecv, kvacc, abuf, qbuf, kgbuf,
+    x_ref, og_ref, wq, wkv, wo, sel, xbuf, gbuf, kvall, kvsend, kvrecv, kvpair, kvacc, abuf, qbuf, kgbuf,
     q3, d3, dt3, a3, qg3, kt, vt, bias,
     part_o, part_q, part_k,
     exo_s, exo_r, exq_s, exq_r, exk_s, exk_r,
@@ -101,9 +101,6 @@
         sent.extend(copies)
         return copies
 
-    def to_seq(peer):
-        return {"seq": peer}
-
     def to_chip(peer):
         return {"seq": peer * 2 + core}
 
@@ -131,15 +128,26 @@
     def columns(index):
         return pl.ds(pl.multiple_of(index * width, 128), width)
 
-    got_g = spread(
-        lambda peer: og_hbm.at[:, columns(peer)], gbuf, chip, chip, chips, to_chip, s_g, r_g
-    )
-
     loads[0].wait()
     loads[1].wait()
     loads[2].wait()
     kvall[me] = jnp.dot(x_ref[...], wkv[...], preferred_element_type=F32).astype(BF16)
-    got_kv = spread(lambda peer: kvall.at[me], kvall, me, me, n_seq, to_seq, s_kv, r_kv)
+    got_kv = spread(lambda peer: kvall.at[me], kvall, me, chip, chips, to_chip, s_kv, r_kv)
+
+    def to_other(source, dest, send_sems, recv_sems, i):
+        copy = pltpu.make_async_remote_copy(
+            src_ref=source, dst_ref=dest, send_sem=send_sems.at[i], recv_sem=recv_sems.at[i],
+            device_id={"seq": chip * 2 + other}, device_id_type=MESH,
+        )
+        copy.start()
+        sent.append(copy)
+        return copy
+
+    got_pair = [to_other(kvall.at[me], kvall.at[me], s_kv, r_kv, chips - 1)]
+
+    got_g = spread(
+        lambda peer: og_hbm.at[:, columns(peer)], gbuf, chip, chip, chips, to_chip, s_g, r_g
+    )
 
     loads[3].wait()
     xbuf[chip] = x_ref[:, columns(chip)]
@@ -149,6 +157,11 @@
     queries = jnp.dot(x_ref[...], wq[...], preferred_element_type=F32)
     for g in range(heads):
         q3[g] = queries[:, g * head : (g + 1) * head].astype(BF16)
+    for k in range(1, chips):
+        got_kv[k - 1].wait_recv()
+        block = kvall.at[lax.rem(chip + chips - k, chips) * 2 + core]
+        got_pair.append(to_other(block, block, s_kv, r_kv, chips - 1 + k))
+
     loads[5].wait()
     for g in range(heads):
         grad_t = lax.dot_general(
@@ -165,7 +178,7 @@
         bias[j * tokens : (j + 1) * tokens, :] = jnp.where(gap <= reach, 0.0, -jnp.inf)
 
     kvacc[...] = jnp.zeros_like(kvacc)
-    arrive(got_kv)
+    arrive(got_pair)
     for j in range(n_seq):
         rows = slice(j * tokens, (j + 1) * tokens)
         kt[:, rows] = kvall[j, :, 0:head].astype(F32).T.astype(BF16)
@@ -198,14 +211,24 @@
     got_a = over_chips(abuf, s_a, r_a)
     for j in range(n_seq):
         rows = slice(j * tokens, (j + 1) * tokens)
-        kvsend[j, :, 0:head] = (kvacc[rows, 0:head] * scale).astype(BF16)
-        kvsend[j, :, head : 2 * head] = kvacc[rows, head : 2 * head].astype(BF16)
+        kvsend[j % 2, j // 2, :, 0:head] = (kvacc[rows, 0:head] * scale).astype(BF16)
+        kvsend[j % 2, j // 2, :, head : 2 * head] = kvacc[rows, head : 2 * head].astype(BF16)
+    got_kx = to_other(kvsend.at[other], kvrecv.at[pl.ds(0, chips)], s_kr, r_kr, chips - 1)
     for g in range(heads):
         qbuf[chip, :, g * head : (g + 1) * head] = qg3[g]
 
     arrive(got_g)
     arrive(got_a)
-    got_kr = spread(lambda peer: kvsend.at[peer], kvrecv, me, me, n_seq, to_seq, s_kr, r_kr)
+    got_kx.wait_recv()
+    for c in range(chips):
+        rows = pl.ds(pl.multiple_of((c * 2 + core) * tokens, tokens), tokens)
+        key_pair = kvacc[rows, 0:head] * scale + kvrecv[c, :, 0:head].astype(F32)
+        value_pair = kvacc[rows, head : 2 * head] + kvrecv[c, :, head : 2 * head].astype(F32)
+        kvpair[c, :, 0:head] = key_pair.astype(BF16)
+        kvpair[c, :, head : 2 * head] = value_pair.astype(BF16)
+    got_kr = spread(
+        lambda peer: kvpair.at[peer], kvrecv, chips + chip, chip, chips, to_chip, s_kr, r_kr
+    )
     got_x = spread(
         lambda peer: x_hbm.at[:, columns(peer)], xbuf, chip, chip, chips, to_chip, s_x, r_x
     )
@@ -233,10 +256,10 @@
 
     arrive(got_kr)
     own = pl.ds(pl.multiple_of(me * tokens, tokens), tokens)
-    key_sum = kvacc[own, 0:head] * scale
-    value_sum = kvacc[own, head : 2 * head]
-    for k in range(1, n_seq):
-        peer = lax.rem(me + k, n_seq)
+    key_sum = kvacc[own, 0:head] * scale + kvrecv[chip, :, 0:head].astype(F32)
+    value_sum = kvacc[own, head : 2 * head] + kvrecv[chip, :, head : 2 * head].astype(F32)
+    for k in range(1, chips):
+        peer = chips + lax.rem(chip + k, chips)
         key_sum += kvrecv[peer, :, 0:head].astype(F32)
         value_sum += kvrecv[peer, :, head : 2 * head].astype(F32)
     kgbuf[chip, :, 0:head] = key_sum.astype(BF16)
@@ -320,8 +343,9 @@
         vmem((depth, q_width), BF16), vmem((depth, 2 * head), BF16), vmem((q_width, depth), BF16),
         vmem((q_width, 2 * side), BF16),
         vmem((chips, tokens, width), BF16), vmem((chips, tokens, width), BF16),
-        vmem((n_seq, tokens, 2 * head), BF16), vmem((n_seq, tokens, 2 * head), BF16),
-        vmem((n_seq, tokens, 2 * head), BF16), vmem((length, 2 * head), F32),
+        vmem((n_seq, tokens, 2 * head), BF16), vmem((2, chips, tokens, 2 * head), BF16),
+        vmem((n_seq, tokens, 2 * head), BF16), vmem((chips, tokens, 2 * head), BF16),
+        vmem((length, 2 * head), F32),
         vmem((chips, tokens, 2 * side), BF16), vmem((chips, tokens, q_width), BF16),
         vmem((chips, tokens, 2 * head), BF16),
     ]

time: 108 us -> 95.4 us (0.88)
  Pallas kernels: 105 us -> 91.8 us
    pallas_call x1, Pallas kernels: 105 us -> 91.8 us  [shards(): pl.pallas_call(functools.partial(kernel, n_seq, n_dp), out_shape=(jax.Sha...]
where the time goes in v3:
time: 95.4 us; the launch traced here: 95.2 us
  Pallas kernels  91.8 us (96%)
  local copies, waits for them, and re-layouts  2.74 us (3%)
    pallas_call x1, Pallas kernels, shards(): pl.pallas_call(functools.partial(kernel, n_seq, n_dp), out_shape=(jax.Sha...  91.8 us
    unnamed x4, local copies, waits for them, and re-layouts  2.74 us

profile of v3, /device:TPU:1, one launch (start us, length us, event | category | flops | bytes accessed | tf_op | source)
XLA Modules:
  0.0 95.2 jit_solution(11850038309966953061)
XLA Ops:
  0.6 91.8 %shard_map.95 = (f32[160,896]{1,0:T(8,128)}, f32[20,5120]{1,0:T(8,128)}) custom-call(bf16[128,5120]{1,0:T(8,128)(2,1)} %bitcast.3, bf16[128,5120]{1,0:T(8,128)(2,1)} %bitcast.4, bf16[5120,640]{1,0:T(8,128)(2,1)} %wq_hbm.1, bf16[5120,128]{1,0:T(8,128)(2,1)} %wk_hbm.1, bf16[5120,128]{1,0:T(8,128)(2,1)} %wv_hbm.1, bf16[640,5120]{1,0:T(8,128)(2,1)} %wo_hbm.1, ...), custom_call_target="tpu_custom_call" | custom-call | tf_op jit(solution)/shard_map/pallas_call | solution.py:368
  92.4 0.0 copy-start
  92.4 2.0 %copy.12 = f32[160,896]{1,0:T(8,128)} copy(f32[160,896]{1,0:T(8,128)} %get-tuple-element.4) | data formatting | bytes 1146880
  94.4 0.0 copy-done
  94.4 0.8 copy.13
Async XLA Ops:
  92.4 2.0 %copy-start = (f32[20,5120]{1,0:T(8,128)S(1)}, f32[20,5120]{1,0:T(8,128)}, u32[]{:S(2)}) copy-start(f32[20,5120]{1,0:T(8,128)} %get-tuple-element.5) | copy-start | bytes 1228804

commit v4 on v3

--- a/solution.py
+++ b/solution.py
@@ -209,16 +209,17 @@
     attn = jnp.concatenate([a3[g] for g in range(heads)], axis=1)
     abuf[chip] = jnp.dot(attn, sel[...], preferred_element_type=F32).astype(BF16)
     got_a = over_chips(abuf, s_a, r_a)
+    for g in range(heads):
+        qbuf[chip, :, g * head : (g + 1) * head] = qg3[g]
+    got_q = over_chips(qbuf, s_q, r_q)
     for j in range(n_seq):
         rows = slice(j * tokens, (j + 1) * tokens)
         kvsend[j % 2, j // 2, :, 0:head] = (kvacc[rows, 0:head] * scale).astype(BF16)
         kvsend[j % 2, j // 2, :, head : 2 * head] = kvacc[rows, head : 2 * head].astype(BF16)
     got_kx = to_other(kvsend.at[other], kvrecv.at[pl.ds(0, chips)], s_kr, r_kr, chips - 1)
-    for g in range(heads):
-        qbuf[chip, :, g * head : (g + 1) * head] = qg3[g]
-
-    arrive(got_g)
-    arrive(got_a)
+    got_x = spread(
+        lambda peer: x_hbm.at[:, columns(peer)], xbuf, chip, chip, chips, to_chip, s_x, r_x
+    )
     got_kx.wait_recv()
     for c in range(chips):
         rows = pl.ds(pl.multiple_of((c * 2 + core) * tokens, tokens), tokens)
@@ -229,10 +230,9 @@
     got_kr = spread(
         lambda peer: kvpair.at[peer], kvrecv, chips + chip, chip, chips, to_chip, s_kr, r_kr
     )
-    got_x = spread(
-        lambda peer: x_hbm.at[:, columns(peer)], xbuf, chip, chip, chips, to_chip, s_x, r_x
-    )
-    got_q = over_chips(qbuf, s_q, r_q)
+
+    arrive(got_g)
+    arrive(got_a)
     group = exo_s.shape[1]
     side = n_dp * group
     grads = gbuf[...].reshape(chips * tokens, width)

time: 95.4 us -> 93.4 us (0.979)
  Pallas kernels: 91.8 us -> 89.3 us
    pallas_call x1, Pallas kernels: 91.8 us -> 89.3 us  [shards(): pl.pallas_call(functools.partial(kernel, n_seq, n_dp), out_shape=(jax.Sha...]
where the time goes in v4:
time: 93.4 us; the launch traced here: 92.7 us
  Pallas kernels  89.3 us (96%)
  local copies, waits for them, and re-layouts  2.74 us (3%)
    pallas_call x1, Pallas kernels, shards(): pl.pallas_call(functools.partial(kernel, n_seq, n_dp), out_shape=(jax.Sha...  89.3 us
    unnamed x4, local copies, waits for them, and re-layouts  2.74 us

profile of v4, /device:TPU:1, one launch (start us, length us, event | category | flops | bytes accessed | tf_op | source)
XLA Modules:
  0.0 92.7 jit_solution(12515968859494129144)
XLA Ops:
  0.6 89.3 %shard_map.95 = (f32[160,896]{1,0:T(8,128)}, f32[20,5120]{1,0:T(8,128)}) custom-call(bf16[128,5120]{1,0:T(8,128)(2,1)} %bitcast.3, bf16[128,5120]{1,0:T(8,128)(2,1)} %bitcast.4, bf16[5120,640]{1,0:T(8,128)(2,1)} %wq_hbm.1, bf16[5120,128]{1,0:T(8,128)(2,1)} %wk_hbm.1, bf16[5120,128]{1,0:T(8,128)(2,1)} %wv_hbm.1, bf16[640,5120]{1,0:T(8,128)(2,1)} %wo_hbm.1, ...), custom_call_target="tpu_custom_call" | custom-call | tf_op jit(solution)/shard_map/pallas_call | solution.py:368
  90.0 0.0 copy-start
  90.0 2.0 %copy.12 = f32[160,896]{1,0:T(8,128)} copy(f32[160,896]{1,0:T(8,128)} %get-tuple-element.4) | data formatting | bytes 1146880
  92.0 0.0 copy-done
  92.0 0.8 copy.13
Async XLA Ops:
  90.0 2.0 %copy-start = (f32[20,5120]{1,0:T(8,128)S(1)}, f32[20,5120]{1,0:T(8,128)}, u32[]{:S(2)}) copy-start(f32[20,5120]{1,0:T(8,128)} %get-tuple-element.5) | copy-start | bytes 1228804

commit v5 on v4

--- a/solution.py
+++ b/solution.py
@@ -184,7 +184,7 @@
         kt[:, rows] = kvall[j, :, 0:head].astype(F32).T.astype(BF16)
         vt[:, rows] = kvall[j, :, head : 2 * head].astype(F32).T.astype(BF16)
 
-    @pl.loop(0, heads)
+    @pl.loop(0, heads, unroll=heads)
     def _(g):
         keys = kvall[:, :, 0:head].reshape(length, head)
         values = kvall[:, :, head : 2 * head].reshape(length, head)

time: 93.4 us -> 92.4 us (0.989)
  no operation moved by 1% of the time
where the time goes in v5:
time: 92.4 us; the launch traced here: 92.2 us
  Pallas kernels  88.8 us (96%)
  local copies, waits for them, and re-layouts  2.74 us (3%)
    pallas_call x1, Pallas kernels, shards(): pl.pallas_call(functools.partial(kernel, n_seq, n_dp), out_shape=(jax.Sha...  88.8 us
    unnamed x4, local copies, waits for them, and re-layouts  2.74 us

profile of v5, /device:TPU:1, one launch (start us, length us, event | category | flops | bytes accessed | tf_op | source)
XLA Modules:
  0.0 92.2 jit_solution(1214720426739349115)
XLA Ops:
  0.6 88.8 %shard_map.95 = (f32[160,896]{1,0:T(8,128)}, f32[20,5120]{1,0:T(8,128)}) custom-call(bf16[128,5120]{1,0:T(8,128)(2,1)} %bitcast.3, bf16[128,5120]{1,0:T(8,128)(2,1)} %bitcast.4, bf16[5120,640]{1,0:T(8,128)(2,1)} %wq_hbm.1, bf16[5120,128]{1,0:T(8,128)(2,1)} %wk_hbm.1, bf16[5120,128]{1,0:T(8,128)(2,1)} %wv_hbm.1, bf16[640,5120]{1,0:T(8,128)(2,1)} %wo_hbm.1, ...), custom_call_target="tpu_custom_call" | custom-call | tf_op jit(solution)/shard_map/pallas_call | solution.py:368
  89.5 0.0 copy-start
  89.5 2.0 %copy.12 = f32[160,896]{1,0:T(8,128)} copy(f32[160,896]{1,0:T(8,128)} %get-tuple-element.4) | data formatting | bytes 1146880
  91.4 0.0 copy-done
  91.4 0.8 copy.13
Async XLA Ops:
  89.5 2.0 %copy-start = (f32[20,5120]{1,0:T(8,128)S(1)}, f32[20,5120]{1,0:T(8,128)}, u32[]{:S(2)}) copy-start(f32[20,5120]{1,0:T(8,128)} %get-tuple-element.5) | copy-start | bytes 1228804
